TPU v7x, 512 devices: a whole 4x4x16 slice. The times are simulated.
512 devices in a mesh: row: 16 (over y, x), col: 16 (over z), depth: 2 (over core).
Axes of the slice: x: 4, y: 4, z: 16, core: 2. Of those that a mesh axis runs over, the one named last changes fastest.
Arguments:
- features: bfloat16 [2, 16384, 1024], P('depth', ('row', 'col')), may hold values from -1.0546875 to 1.0546875
Outputs:
- drift: float32 [16384, 16384], P(('row', 'depth'), 'col')
All inputs are finite; a program needn't handle non-finite values.
Results may differ from a plain program's by a relative error of at most 0.0003.
Values may be sent and summed in bfloat16 or wider, within the bound.
No kernel may reach another device: no remote copies, remote signals or barrier semaphores. Data moves between devices by JAX's collectives and lax.ppermute only.
A program may use at most 64 MiB of HBM per device.

v0:
```python
import jax
import jax.numpy as jnp
from jax import lax
from jax.sharding import PartitionSpec as P


def broadcast(value, axis, source):
    kept = jnp.where(lax.axis_index(axis) == source, value, 0).astype(value.dtype)
    return lax.psum(kept, axis)


def transposed_product(left_rows, right_rows):
    return lax.dot_general(
        left_rows, right_rows, (((1,), (1,)), ((), ())), preferred_element_type=jnp.float32
    )


def body(features):
    rows_of = lax.axis_size("row")
    cols_of = lax.axis_size("col")
    own_shard = features[0]
    ex_dev = own_shard.shape[0]
    feat_width = own_shard.shape[1]
    per_dest = ex_dev // cols_of
    grouped = own_shard.reshape(cols_of, per_dest, 1, feat_width)
    row_piece = lax.all_to_all(grouped, "col", split_axis=0, concat_axis=2, tiled=True)
    row_block = lax.all_gather(row_piece.reshape(ex_dev, feat_width), "col", axis=0, tiled=True)
    col_ratio = cols_of // rows_of
    col_index = lax.axis_index("col")
    col_block = broadcast(row_block, "row", col_index // col_ratio)
    depth_index = lax.axis_index("depth")
    signum = 2.0 * depth_index.astype(jnp.float32) - 1.0
    return lax.psum_scatter(
        signum * transposed_product(row_block, col_block), "depth", scatter_dimension=0, tiled=True
    )


def solution(mesh):
    placed = (P("depth", ("row", "col"), None),)
    return jax.shard_map(
        body, mesh=mesh, in_specs=placed, out_specs=P(("row", "depth"), "col"), check_vma=False
    )
```

profile of v0, /device:TPU:1, one launch (start us, length us, event | category | flops | bytes accessed | tf_op | source)
XLA Modules:
  0.0 265.4 jit_solution(9115069896049042623)
XLA Ops:
  6.5 0.0 all-gather.2.cloned.1.call-start
  6.5 1.0 reshape_squeeze.3
  7.5 27.5 %all_to_all.15 = bf16[16,4,1,1024]{3,1,2,0:T(4,128)(2,1)S(1)} all-to-all(bf16[16,4,1,1024]{3,1,2,0:T(4,128)(2,1)S(1)} %bitcast.11), channel_id=1, replica_groups=mesh['row'=16,'col'=16,'depth'=2] {'col'}, dimensions={0} | all-to-all | bytes 262144 | tf_op jit(solution)/shard_map/all_to_all | solution.py:26
  35.0 0.7 copy.7
  35.7 0.0 all-gather.2.cloned.1.call-update
  35.8 0.0 all-reduce.2.cloned.1.call-start
  35.8 60.2 %all-gather.2.cloned.1.call-done = bf16[1024,1024]{1,0:T(8,128)(2,1)} async-done(((bf16[64,1024]{1,0:T(8,128)(2,1)}), bf16[1024,1024]{1,0:T(8,128)(2,1)}) %all-gather.2.cloned.1.call-update) | async-done | bytes 2097168 | tf_op jit(solution)/shard_map/all_gather | solution.py:27
  96.1 3.0 %broadcast_select_fusion = bf16[1024,1024]{1,0:T(8,128)(2,1)} fusion(bf16[1024,1024]{1,0:T(8,128)(2,1)} %all-gather.2.cloned.1.call-done, pred[]{:T(512)S(6)} %eq.3), kind=kLoop, calls=%fused_computation.1 | loop fusion | flops 1048576 | bytes 4194305 | tf_op jit(solution)/shard_map/jit(_where)/select_n | solution.py:8
  99.1 0.0 copy-start
  99.1 0.0 all-reduce.2.cloned.1.call-update
  99.1 0.0 reduce-scatter.2.cloned.1.call-start
  99.2 126.3 %all-reduce.2.cloned.1.call-done = bf16[1024,1024]{1,0:T(8,128)(2,1)} async-done(((bf16[1024,1024]{1,0:T(8,128)(2,1)}), bf16[1024,1024]{1,0:T(8,128)(2,1)}) %all-reduce.2.cloned.1.call-update) | async-done | bytes 2097168 | tf_op jit(solution)/shard_map/psum | solution.py:9
  225.5 0.0 copy-done
  225.5 5.9 %multiply_bitcast_fusion = f32[1024,1024]{0,1:T(8,128)} fusion(bf16[1024,1024]{1,0:T(8,128)(2,1)} %all-reduce.2.cloned.1.call-done, bf16[1024,1024]{1,0:T(8,128)(2,1)S(1)} %copy-done, f32[]{:T(128)S(6)} %sub.5), kind=kOutput, calls=%fused_computation | convolution fusion | flops 2148532224 | bytes 8388612 | tf_op jit(solution)/shard_map/dot_general | solution.py:13
  231.4 0.0 reduce-scatter.2.cloned.1.call-update
  231.4 24.6 %reduce-scatter.2.cloned.1.call-done = f32[512,1024]{0,1:T(8,128)} async-done(((f32[1024,1024]{0,1:T(8,128)}), f32[512,1024]{0,1:T(8,128)}) %reduce-scatter.2.cloned.1.call-update) | async-done | bytes 2097168 | tf_op jit(solution)/shard_map/reduce_scatter | solution.py:33
  256.0 2.9 %copy.8 = f32[512,1024]{1,0:T(8,128)} copy(f32[512,1024]{0,1:T(8,128)} %reduce-scatter.2.cloned.1.call-done) | data formatting | bytes 4194304 | tf_op jit(solution)/shard_map/reduce_scatter | solution.py:33
Async XLA Ops:
  6.5 89.5 %all-gather.2.cloned.1.call-start = ((), (), s32[]{:S(2)}) async-start(), calls=%async_computation.2 | async-start | bytes 2228224 | tf_op jit(solution)/shard_map/all_gather | solution.py:27
  35.8 189.7 %all-reduce.2.cloned.1.call-start = ((), (), s32[]{:S(2)}) async-start(), calls=%async_computation.3 | async-start | bytes 4194304 | tf_op jit(solution)/shard_map/psum | solution.py:9
  99.1 126.4 %copy-start = (bf16[1024,1024]{1,0:T(8,128)(2,1)S(1)}, bf16[1024,1024]{1,0:T(8,128)(2,1)}, u32[]{:S(2)}) copy-start(bf16[1024,1024]{1,0:T(8,128)(2,1)} %all-gather.2.cloned.1.call-done) | copy-start | bytes 6291460
  99.1 156.8 %reduce-scatter.2.cloned.1.call-start = ((), (), s32[]{:S(2)}) async-start(), calls=%async_computation.4 | async-start | bytes 6291456 | tf_op jit(solution)/shard_map/reduce_scatter | solution.py:33
Sparse Core Ops, SparseCore 0:
  35.9 60.1 all-gather.1
  99.4 126.0 all-reduce.1
  231.5 24.4 reduce-scatter.1
where the time goes:
time: 266 us; the launch traced here: 265 us
  waiting for transfers between devices  211 us (79%)
  blocking collectives  27.5 us (10%)
  between operations  13.1 us (5%)
  matrix products  5.9 us (2%)
  local copies, waits for them, and re-layouts  4.54 us (2%)
  other arithmetic  3.05 us (1%)
    psum x1, waiting for transfers between devices, broadcast(): return lax.psum(kept, axis)  126 us
    all_gather x1, waiting for transfers between devices, body(): lax.all_gather(row_piece.reshape(ex_dev, feat_width), 'col', axis=0, tile...  60.2 us
    all_to_all x1, blocking collectives, body(): lax.all_to_all(grouped, 'col', split_axis=0, concat_axis=2, tiled=True)  27.5 us
    reduce_scatter x1, waiting for transfers between devices, body(): lax.psum_scatter(signum * transposed_product(row_block, col_block), 'dept...  24.6 us
    dot_general x1, matrix products, transposed_product(): lax.dot_general(left_rows, right_rows, (((1,), (1,)), ((), ())), preferre...  5.9 us
  transfers between devices with their start and end apart: 3, of which 3 were waited for; matrix products, arithmetic and copies ran while one was open for 0% of the time, Pallas kernels for 0%

commit v1 on v0

--- a/solution.py
+++ b/solution.py
@@ -6,7 +6,7 @@
 
 def broadcast(value, axis, source):
     kept = jnp.where(lax.axis_index(axis) == source, value, 0).astype(value.dtype)
-    return lax.psum(kept, axis)
+    return jnp.sum(lax.all_gather(kept, axis), axis=0)
 
 
 def transposed_product(left_rows, right_rows):

time: 266 us -> 369 us (1.39)
  waiting for transfers between devices: 211 us -> 303 us
  other arithmetic: 3.05 us -> 14.8 us
    all_gather x0 -> x1, waiting for transfers between devices: none -> 218 us  [broadcast(): return jnp.sum(lax.all_gather(kept, axis), axis=0)]
    psum x1 -> x0, waiting for transfers between devices: 126 us -> none  [broadcast(): return lax.psum(kept, axis)]
    reduce_sum x0 -> x1, other arithmetic: none -> 11.7 us  [broadcast(): return jnp.sum(lax.all_gather(kept, axis), axis=0)]
where the time goes in v1:
time: 369 us
  waiting for transfers between devices  303 us (82%)
  blocking collectives  27.5 us (7%)
  other arithmetic  14.8 us (4%)
  between operations  13.1 us (4%)
  matrix products  5.9 us (2%)
  local copies, waits for them, and re-layouts  4.54 us (1%)
    all_gather x1, waiting for transfers between devices, broadcast(): return jnp.sum(lax.all_gather(kept, axis), axis=0)  218 us
    all_gather x1, waiting for transfers between devices, body(): lax.all_gather(row_piece.reshape(ex_dev, feat_width), 'col', axis=0, tile...  60.2 us
    all_to_all x1, blocking collectives, body(): lax.all_to_all(grouped, 'col', split_axis=0, concat_axis=2, tiled=True)  27.5 us
    reduce_scatter x1, waiting for transfers between devices, body(): lax.psum_scatter(signum * transposed_product(row_block, col_block), 'dept...  23.8 us
    reduce_sum x1, other arithmetic, broadcast(): return jnp.sum(lax.all_gather(kept, axis), axis=0)  11.7 us
  transfers between devices with their start and end apart: 3, of which 3 were waited for; matrix products, arithmetic and copies ran while one was open for 0% of the time, Pallas kernels for 0%

profile of v1, /device:TPU:1, one launch (start us, length us, event | category | flops | bytes accessed | tf_op | source)
XLA Modules:
  0.0 368.5 jit_solution(10441704763632106798)
XLA Ops:
  6.5 0.0 all-gather.4.cloned.1.call-start
  6.5 1.0 reshape_squeeze.3
  7.5 27.5 %all_to_all.15 = bf16[16,4,1,1024]{3,1,2,0:T(4,128)(2,1)S(1)} all-to-all(bf16[16,4,1,1024]{3,1,2,0:T(4,128)(2,1)S(1)} %bitcast.13), channel_id=1, replica_groups=mesh['row'=16,'col'=16,'depth'=2] {'col'}, dimensions={0} | all-to-all | bytes 262144 | tf_op jit(solution)/shard_map/all_to_all | solution.py:26
  35.0 0.7 copy.7
  35.7 0.0 all-gather.4.cloned.1.call-update
  35.8 0.0 all-gather.6.cloned.1.call-start
  35.8 60.2 %all-gather.4.cloned.1.call-done = bf16[1024,1024]{1,0:T(8,128)(2,1)} async-done(((bf16[64,1024]{1,0:T(8,128)(2,1)}), bf16[1024,1024]{1,0:T(8,128)(2,1)}) %all-gather.4.cloned.1.call-update) | async-done | bytes 2097168 | tf_op jit(solution)/shard_map/all_gather | solution.py:27
  96.1 3.0 broadcast_select_fusion
  99.1 0.0 all-gather.6.cloned.1.call-update
  99.1 0.0 reduce-scatter.2.cloned.1.call-start
  99.2 218.4 %all-gather.6.cloned.1.call-done = bf16[16384,1024]{1,0:T(8,128)(2,1)} async-done(((bf16[1024,1024]{1,0:T(8,128)(2,1)}), bf16[16384,1024]{1,0:T(8,128)(2,1)}) %all-gather.6.cloned.1.call-update) | async-done | bytes 33554448 | tf_op jit(solution)/shard_map/all_gather | solution.py:9
  317.6 11.7 %reduce_sum.12 = bf16[1024,1024]{1,0:T(8,128)(2,1)S(1)} reduce(bf16[16,1024,1024]{2,1,0:T(8,128)(2,1)} %bitcast.11, bf16[]{:T(256)} %constant.32.clone.1), dimensions={0}, to_apply=%region_0.1 | reduce | flops 15728640 | bytes 35651584 | tf_op jit(solution)/shard_map/reduce_sum | solution.py:9
  329.4 5.9 %multiply_bitcast_fusion = f32[1024,1024]{0,1:T(8,128)} fusion(bf16[1024,1024]{1,0:T(8,128)(2,1)S(1)} %reduce_sum.12, bf16[1024,1024]{1,0:T(8,128)(2,1)} %all-gather.4.cloned.1.call-done, f32[]{:T(128)S(6)} %sub.5), kind=kOutput, calls=%fused_computation | convolution fusion | flops 2148532224 | bytes 8388612 | tf_op jit(solution)/shard_map/dot_general | solution.py:13
  335.3 0.0 reduce-scatter.2.cloned.1.call-update
  335.3 23.8 %reduce-scatter.2.cloned.1.call-done = f32[512,1024]{0,1:T(8,128)} async-done(((f32[1024,1024]{0,1:T(8,128)}), f32[512,1024]{0,1:T(8,128)}) %reduce-scatter.2.cloned.1.call-update) | async-done | bytes 2097168 | tf_op jit(solution)/shard_map/reduce_scatter | solution.py:33
  359.1 2.9 copy.8
Async XLA Ops:
  6.5 89.5 %all-gather.4.cloned.1.call-start = ((), (), s32[]{:S(2)}) async-start(), calls=%async_computation.2 | async-start | bytes 2228224 | tf_op jit(solution)/shard_map/all_gather | solution.py:27
  35.8 281.8 %all-gather.6.cloned.1.call-start = ((), (), s32[]{:S(2)}) async-start(), calls=%async_computation.4 | async-start | bytes 35651584 | tf_op jit(solution)/shard_map/all_gather | solution.py:9
  99.1 260.0 %reduce-scatter.2.cloned.1.call-start = ((), (), s32[]{:S(2)}) async-start(), calls=%async_computation.3 | async-start | bytes 6291456 | tf_op jit(solution)/shard_map/reduce_scatter | solution.py:33
Sparse Core Ops, SparseCore 0:
  35.9 60.1 all-gather.3
  99.3 218.3 all-gather.5
  335.4 23.6 reduce-scatter.1

commit v2 on v0

--- a/solution.py
+++ b/solution.py
@@ -24,7 +24,12 @@
     per_dest = ex_dev // cols_of
     grouped = own_shard.reshape(cols_of, per_dest, 1, feat_width)
     row_piece = lax.all_to_all(grouped, "col", split_axis=0, concat_axis=2, tiled=True)
-    row_block = lax.all_gather(row_piece.reshape(ex_dev, feat_width), "col", axis=0, tiled=True)
+    row_block = jnp.concatenate(
+        lax.all_to_all(
+            jnp.stack([row_piece.reshape(ex_dev, feat_width)] * lax.axis_size("col")), "col", 0, 0
+        ),
+        axis=0,
+    )
     col_ratio = cols_of // rows_of
     col_index = lax.axis_index("col")
     col_block = broadcast(row_block, "row", col_index // col_ratio)

time: 266 us -> 297 us (1.12)
  waiting for transfers between devices: 211 us -> 237 us
  starting transfers between devices: 0.09 us -> 6.01 us
    all_to_all x0 -> x1, waiting for transfers between devices: none -> 91.8 us  [body(): lax.all_to_all(jnp.stack([row_piece.reshape(ex_dev, feat_width)] * lax.ax...]
    all_gather x1 -> x0, waiting for transfers between devices: 60.2 us -> none  [body(): lax.all_gather(row_piece.reshape(ex_dev, feat_width), 'col', axis=0, tile...]
    all_to_all x0 -> x1, starting transfers between devices: none -> 5.93 us  [body(): lax.all_to_all(jnp.stack([row_piece.reshape(ex_dev, feat_width)] * lax.ax...]
    psum x1, waiting for transfers between devices: 126 us -> 121 us  [broadcast(): return lax.psum(kept, axis)]
where the time goes in v2:
time: 297 us
  waiting for transfers between devices  237 us (80%)
  blocking collectives  27.5 us (9%)
  between operations  13.4 us (5%)
  starting transfers between devices  6.01 us (2%)
  matrix products  5.9 us (2%)
  local copies, waits for them, and re-layouts  5.47 us (2%)
    psum x1, waiting for transfers between devices, broadcast(): return lax.psum(kept, axis)  121 us
    all_to_all x1, waiting for transfers between devices, body(): lax.all_to_all(jnp.stack([row_piece.reshape(ex_dev, feat_width)] * lax.ax...  91.8 us
    all_to_all x1, blocking collectives, body(): lax.all_to_all(grouped, 'col', split_axis=0, concat_axis=2, tiled=True)  27.5 us
    reduce_scatter x1, waiting for transfers between devices, body(): lax.psum_scatter(signum * transposed_product(row_block, col_block), 'dept...  24.6 us
  transfers between devices with their start and end apart: 3, of which 3 were waited for; matrix products, arithmetic and copies ran while one was open for 0% of the time, Pallas kernels for 0%

profile of v2, /device:TPU:1, one launch (start us, length us, event | category | flops | bytes accessed | tf_op | source)
XLA Modules:
  0.0 296.9 jit_solution(8573551591369787447)
XLA Ops:
  6.5 1.0 reshape_squeeze.3
  7.5 27.5 %all_to_all.20 = bf16[16,4,1,1024]{3,1,2,0:T(4,128)(2,1)S(1)} all-to-all(bf16[16,4,1,1024]{3,1,2,0:T(4,128)(2,1)S(1)} %bitcast.14), channel_id=1, replica_groups=mesh['row'=16,'col'=16,'depth'=2] {'col'}, dimensions={0} | all-to-all | bytes 262144 | tf_op jit(solution)/shard_map/all_to_all | solution.py:26
  35.1 1.6 stack.3
  36.7 5.9 %all-to-all-start.1 = ((bf16[16,64,1024]{2,1,0:T(8,128)(2,1)}), bf16[16,64,1024]{2,1,0:T(8,128)(2,1)S(1)}, u32[]{:S(2)}, u32[]{:S(2)}) async-start(bf16[16,64,1024]{2,1,0:T(8,128)(2,1)} %stack.3), calls=%async_computation.1 | async-start | bytes 4194304 | tf_op jit(solution)/shard_map/all_to_all | solution.py:28
  42.6 0.0 all-reduce.2.cloned.1.call-start
  42.7 91.8 %all-to-all-done.1 = bf16[16,64,1024]{2,1,0:T(8,128)(2,1)S(1)} async-done(((bf16[16,64,1024]{2,1,0:T(8,128)(2,1)}), bf16[16,64,1024]{2,1,0:T(8,128)(2,1)S(1)}, u32[]{:S(2)}, u32[]{:S(2)}) %all-to-all-start.1) | async-done | bytes 2097184 | tf_op jit(solution)/shard_map/all_to_all | solution.py:28
  134.4 1.6 broadcast_select_fusion
  136.0 0.0 all-reduce.2.cloned.1.call-update
  136.1 0.0 reduce-scatter.2.cloned.1.call-start
  136.1 120.5 %all-reduce.2.cloned.1.call-done = bf16[1024,1024]{1,0:T(8,128)(2,1)} async-done(((bf16[1024,1024]{1,0:T(8,128)(2,1)}), bf16[1024,1024]{1,0:T(8,128)(2,1)}) %all-reduce.2.cloned.1.call-update) | async-done | bytes 2097168 | tf_op jit(solution)/shard_map/psum | solution.py:9
  256.7 5.9 %multiply_bitcast_fusion = f32[1024,1024]{0,1:T(8,128)} fusion(bf16[1024,1024]{1,0:T(8,128)(2,1)} %all-reduce.2.cloned.1.call-done, bf16[1024,1024]{1,0:T(8,128)(2,1)S(1)} %bitcast.12, f32[]{:T(128)S(6)} %sub.5), kind=kOutput, calls=%fused_computation | convolution fusion | flops 2148532224 | bytes 8388612 | tf_op jit(solution)/shard_map/dot_general | solution.py:13
  262.6 0.0 reduce-scatter.2.cloned.1.call-update
  262.6 24.6 %reduce-scatter.2.cloned.1.call-done = f32[512,1024]{0,1:T(8,128)} async-done(((f32[1024,1024]{0,1:T(8,128)}), f32[512,1024]{0,1:T(8,128)}) %reduce-scatter.2.cloned.1.call-update) | async-done | bytes 2097168 | tf_op jit(solution)/shard_map/reduce_scatter | solution.py:38
  287.2 2.9 copy.8
  (1 shorter events, 0.0 us)
Async XLA Ops:
  36.7 97.8 %all-to-all-start.1 = ((bf16[16,64,1024]{2,1,0:T(8,128)(2,1)}), bf16[16,64,1024]{2,1,0:T(8,128)(2,1)S(1)}, u32[]{:S(2)}, u32[]{:S(2)}) async-start(bf16[16,64,1024]{2,1,0:T(8,128)(2,1)} %stack.3), calls=%async_computation.1 | async-start | bytes 4194304 | tf_op jit(solution)/shard_map/all_to_all | solution.py:28
  42.6 214.0 %all-reduce.2.cloned.1.call-start = ((), (), s32[]{:S(2)}) async-start(), calls=%async_computation.3 | async-start | bytes 4194304 | tf_op jit(solution)/shard_map/psum | solution.py:9
  136.1 151.1 %reduce-scatter.2.cloned.1.call-start = ((), (), s32[]{:S(2)}) async-start(), calls=%async_computation.4 | async-start | bytes 6291456 | tf_op jit(solution)/shard_map/reduce_scatter | solution.py:38
Sparse Core Ops, SparseCore 0:
  136.2 120.4 all-reduce.1
  262.7 24.4 reduce-scatter.1
